TPU v7x, 256 devices: a whole 4x4x8 slice. The times are simulated.
256 devices in a mesh: ia: 4 (over y), ja: 4 (over x), ka: 16 (over z, core).
Axes of the slice: x: 4, y: 4, z: 8, core: 2. Of those that a mesh axis runs over, the one named last changes fastest.
Arguments:
- blocks: bfloat16 [4, 4, 16, 2, 128, 128, 128], P('ia', 'ja', 'ka'), may hold values from -6 to 6
- first_mode_rows: int32 [4, 4, 16, 2], P('ia', 'ja', 'ka'), may hold values from 0 to 15
- second_mode_rows: int32 [4, 4, 16, 2], P('ia', 'ja', 'ka'), may hold values from 0 to 15
- third_mode_rows: int32 [4, 4, 16, 2], P('ia', 'ja', 'ka'), may hold values from 0 to 3
- filled: int32 [4, 4, 16], P('ia', 'ja', 'ka'), may hold values from 1 to 2, as said below
- owner_one: int32 [64], replicated, may hold values from 0 to 63, each once
- owner_two: int32 [64], replicated, may hold values from 0 to 63, each once
- factor_b: float32 [4, 2048, 256], P('ja', ('ia', 'ka'))
- factor_c: float32 [16, 512, 256], P('ka')
Outputs:
- a_new: float32 [4, 2048, 256], P('ia', ('ja', 'ka'))
- b_new: float32 [4, 2048, 256], P('ja', ('ia', 'ka'))
Inputs may be any that keep to these rules, and one draw needn't show every extreme that they name: Number of nonempty slots of a grid cell; at least one cell has all 2 slots filled. Slots at or beyond this count hold data that is not part of the tensor.
All inputs are finite; a program needn't handle non-finite values.
Results may differ from a plain program's by a relative error of at most 0.0039.
The roundings to bfloat16 on the way count: a program that leaves them out, or rounds other values in their place, can miss the bound.
Values may be sent and summed in bfloat16 or wider, within the bound.
A program may use at most 128 MiB of HBM per device.

v0:
```python
import jax
import jax.numpy as jnp
from jax import lax
from jax.sharding import PartitionSpec as P

EPS = 1e-06


def solve_rows(gram, rows):
    lower = jnp.linalg.cholesky(gram)
    return jax.scipy.linalg.cho_solve((lower, True), rows.T).T


def add_rows(accum, start, contrib):
    current = lax.dynamic_slice_in_dim(accum, start, contrib.shape[0], 0)
    return lax.dynamic_update_slice_in_dim(accum, current + contrib, start, 0)


def batched_sum(inner, weights):
    summed = lax.dot_general(
        inner,
        weights.astype(jnp.float32),
        (((1,), (0,)), ((2,), (1,))),
        precision=lax.Precision.HIGHEST,
        preferred_element_type=jnp.float32,
    )
    return summed.T


def to_logical(stored, owner, piece_rows):
    return stored.reshape(-1, piece_rows, stored.shape[1])[owner].reshape(stored.shape)


def to_stored(logical, owner, piece_rows):
    positions = jnp.arange(owner.shape[0], dtype=jnp.int32)
    inverse = jnp.sum(
        jnp.where(owner[None, :] == positions[:, None], positions[None, :], 0), axis=1
    )
    return logical.reshape(-1, piece_rows, logical.shape[1])[inverse].reshape(logical.shape)


def keep_same(value):
    return value


def partial_value(function, slot):

    def applied(value):
        return function(value, slot)

    return applied


def body(
    blocks,
    first_mode_rows,
    second_mode_rows,
    third_mode_rows,
    filled,
    owner_one,
    owner_two,
    factor_b,
    factor_c,
):
    highest = lax.Precision.HIGHEST
    piece_rows = factor_b.shape[1]
    rank_width = factor_b.shape[2]
    block_edge = blocks.shape[-1]
    slot_count = blocks.shape[3]
    total_one = piece_rows * lax.axis_size("ia") * lax.axis_size("ja") * lax.axis_size("ka")
    slab_rows_one = piece_rows * lax.axis_size("ja") * lax.axis_size("ka")
    slab_rows_two = piece_rows * lax.axis_size("ia") * lax.axis_size("ka")
    own_b = factor_b[0]
    own_c = lax.dynamic_slice_in_dim(
        factor_c[0], lax.axis_index(("ia", "ja")) * piece_rows, piece_rows, 0
    )
    local_b = jnp.dot(own_b.T, own_b, precision=highest, preferred_element_type=jnp.float32)
    local_c = jnp.dot(own_c.T, own_c, precision=highest, preferred_element_type=jnp.float32)
    gram_b, gram_c = lax.psum((local_b, local_c), ("ia", "ja", "ka"))
    stored_b = lax.all_gather(factor_b.astype(jnp.bfloat16), ("ia", "ka"), axis=1, tiled=True)[0]
    half_b = to_logical(stored_b, owner_two, piece_rows)
    half_c = factor_c[0].astype(jnp.bfloat16)
    live_count = filled[0, 0, 0]

    def update_one(partial_sum, slot):
        block = blocks[0, 0, 0, slot]
        b_rows = lax.dynamic_slice_in_dim(
            half_b, second_mode_rows[0, 0, 0, slot] * block_edge, block_edge, 0
        )
        c_rows = lax.dynamic_slice_in_dim(
            half_c, third_mode_rows[0, 0, 0, slot] * block_edge, block_edge, 0
        )
        inner = jnp.dot(
            block.reshape(block_edge * block_edge, block_edge),
            c_rows,
            preferred_element_type=jnp.float32,
        )
        inner = inner.reshape(block_edge, block_edge, rank_width)
        contrib = batched_sum(inner, b_rows)
        return add_rows(partial_sum, first_mode_rows[0, 0, 0, slot] * block_edge, contrib)

    partial_one = jnp.zeros((slab_rows_one, rank_width), jnp.float32)
    for slot in range(slot_count):
        partial_one = lax.cond(
            slot < live_count, partial_value(update_one, slot), keep_same, partial_one
        )
    stored_one = to_stored(partial_one, owner_one, piece_rows)
    system_one = gram_b * gram_c
    summed_own = lax.psum_scatter(stored_one, ("ja", "ka"), scatter_dimension=0, tiled=True)
    a_hat = solve_rows(system_one, summed_own)
    squares_a = lax.psum(jnp.sum(a_hat * a_hat, axis=0), ("ia", "ja", "ka"))
    scale_a = jnp.sqrt(squares_a / total_one + EPS)
    a_own = a_hat / scale_a
    local_a = jnp.dot(a_own.T, a_own, precision=highest, preferred_element_type=jnp.float32)
    gram_a = lax.psum(local_a, ("ia", "ja", "ka"))
    stored_a = lax.all_gather(a_own.astype(jnp.bfloat16)[None], ("ja", "ka"), axis=1, tiled=True)[0]
    half_a = to_logical(stored_a, owner_one, piece_rows)

    def update_two(partial_sum, slot):
        block = blocks[0, 0, 0, slot]
        a_rows = lax.dynamic_slice_in_dim(
            half_a, first_mode_rows[0, 0, 0, slot] * block_edge, block_edge, 0
        )
        c_rows = lax.dynamic_slice_in_dim(
            half_c, third_mode_rows[0, 0, 0, slot] * block_edge, block_edge, 0
        )
        inner = lax.dot_general(
            block.reshape(block_edge, block_edge * block_edge),
            a_rows,
            (((0,), (0,)), ((), ())),
            preferred_element_type=jnp.float32,
        )
        inner = inner.reshape(block_edge, block_edge, rank_width)
        contrib = batched_sum(inner, c_rows)
        return add_rows(partial_sum, second_mode_rows[0, 0, 0, slot] * block_edge, contrib)

    partial_two = jnp.zeros((slab_rows_two, rank_width), jnp.float32)
    for slot in range(slot_count):
        partial_two = lax.cond(
            slot < live_count, partial_value(update_two, slot), keep_same, partial_two
        )
    stored_two = to_stored(partial_two, owner_two, piece_rows)
    summed_two = lax.psum_scatter(stored_two, ("ia", "ka"), scatter_dimension=0, tiled=True)
    b_hat = solve_rows(gram_a * gram_c, summed_two)
    squares_b = lax.psum(jnp.sum(b_hat * b_hat, axis=0), ("ia", "ja", "ka"))
    b_own = b_hat / jnp.sqrt(squares_b / total_one + EPS)
    return (a_own[None], b_own[None])


def solution(mesh):
    return jax.shard_map(
        body,
        mesh=mesh,
        in_specs=(
            P("ia", "ja", "ka", None, None, None, None),
            P("ia", "ja", "ka", None),
            P("ia", "ja", "ka", None),
            P("ia", "ja", "ka", None),
            P("ia", "ja", "ka"),
            P(),
            P(),
            P("ja", ("ia", "ka"), None),
            P("ka", None, None),
        ),
        out_specs=(P("ia", ("ja", "ka"), None), P("ja", ("ia", "ka"), None)),
        check_vma=False,
    )
```

profile of v0, /device:TPU:1, one launch (start us, length us, event | category | flops | bytes accessed | tf_op | source)
XLA Modules:
  0.0 827.5 jit_solution(4852424667202017735)
XLA Ops:
  9.5 2.0 fusion.34
  11.5 2.0 fusion.36
  17.5 75.5 %all-gather.4.cloned.1.call-done = bf16[1,2048,256]{2,1,0:T(8,128)(2,1)} async-done(((bf16[1,32,256]{2,1,0:T(8,128)(2,1)}), bf16[1,2048,256]{2,1,0:T(8,128)(2,1)}) %all-gather.4.cloned.1.call-update) | async-done | bytes 1048592 | tf_op jit(solution)/shard_map/all_gather | solution.py:80
  93.0 1.8 gather_fusion
  94.8 23.3 %conditional.4 = (f32[2048,256]{1,0:T(8,128)}) conditional(s32[]{:T(128)} %bitcast.41, () %tuple.54, (s32[1,1,1,2]{3,2,1,0:T(1,128)}, bf16[512,256]{1,0:T(8,128)(2,1)S(1)}, bf16[1,1,1,2,128,128,128]{6,5,4,3,2,1,0:T(8,128)(2,1)}, s32[1,1,1,2]{3,2,1,0:T(1,128)}, bf16[2048,256]{1,0:T(8,128)(2,1)S(1)}, /*index=5*/s32[1,1,1,2]{3,2,1,0:T(1,128)}) %tuple.134), branch_computations={%region_6.0_spmd, %region_7.0_spmd} | conditional | flops 1082130432 | bytes 83099928 | solution.py:104
  95.5 2.8 slice.76
  98.3 2.4 convolution_bitcast_fusion
  100.7 6.7 copy.52
  107.6 8.2 multiply_reduce_fusion
  118.1 3.6 gather_fusion.1
  122.1 149.6 %all-reduce.7.cloned.1.call-done = (f32[256,256]{0,1:T(8,128)}, f32[256,256]{0,1:T(8,128)}) async-done(((f32[256,256]{0,1:T(8,128)}, f32[256,256]{0,1:T(8,128)}), (f32[256,256]{0,1:T(8,128)}, f32[256,256]{0,1:T(8,128)})) %all-reduce.7.cloned.1.call-update) | async-done | bytes 524304 | tf_op jit(solution)/shard_map/psum | solution.py:79
  272.9 11.7 %cholesky.130 = f32[128,128]{1,0:T(8,128)S(1)} custom-call(f32[128,128]{1,0:T(8,128)S(1)} %cholesky.194), custom_call_target="Cholesky" | custom-call | tf_op jit(solution)/shard_map/jit(cholesky)/cholesky | solution.py:10
  284.7 9.8 %custom-call.15 = f32[1,128,128]{1,2,0:T(8,128)S(1)} custom-call(f32[1,128,128]{2,1,0:T(8,128)S(1)} %get-tuple-element.155), custom_call_target="InvertDiagBlocksLowerTriangular" | custom-call | tf_op jit(solution)/shard_map/jit(cholesky)/cholesky | solution.py:10
  295.0 11.7 %cholesky.147 = f32[128,128]{1,0:T(8,128)S(1)} custom-call(f32[128,128]{1,0:T(8,128)S(1)} %convolution_subtract_fusion.1), custom_call_target="Cholesky" | custom-call | tf_op jit(solution)/shard_map/jit(cholesky)/cholesky | solution.py:10
  308.8 14.6 %while.4 = (s32[]{:T(128)}, f32[256,256]{1,0:T(8,128)S(1)}, s32[2,2]{1,0:T(2,128)S(1)}, f32[2,128,128]{2,1,0:T(8,128)S(1)}, s32[]{:T(128)}) while((s32[]{:T(128)}, f32[256,256]{1,0:T(8,128)S(1)}, s32[2,2]{1,0:T(2,128)S(1)}, f32[2,128,128]{2,1,0:T(8,128)S(1)}, s32[]{:T(128)}) %tuple.103), condition=%wide.while_cond, body=%wide.while_body.sunk | while | flops 2 | bytes 131181 | solution.py:11
  323.4 19.7 %custom-call.16 = f32[2,128,128]{1,2,0:T(8,128)S(1)} custom-call(f32[2,128,128]{2,1,0:T(8,128)S(1)} %get-tuple-element.124), custom_call_target="InvertDiagBlocksLowerTriangular" | custom-call | tf_op jit(solution)/shard_map/jit(_cho_solve)/triangular_solve | solution.py:11
  345.9 77.9 %psum.37 = f32[256]{0:T(256)S(1)} all-reduce(f32[256]{0:T(256)S(1)} %multiply_reduce_fusion.5), channel_id=1, replica_groups=mesh['ia'=4,'ja'=4,'ka'=16] {'ia','ja','ka'}, use_global_device_ids=true, to_apply=%region_13.16 | all-reduce | flops 256 | bytes 2048 | tf_op jit(solution)/shard_map/psum | solution.py:111
  425.8 71.7 %all-gather.6.cloned.1.call-done = bf16[2048,256]{1,0:T(8,128)(2,1)} async-done(((bf16[32,256]{1,0:T(8,128)(2,1)}), bf16[2048,256]{1,0:T(8,128)(2,1)}) %all-gather.6.cloned.1.call-update) | async-done | bytes 1048592 | tf_op jit(solution)/shard_map/all_gather | solution.py:116
  497.5 1.8 gather_fusion.2
  499.4 23.6 %conditional.6 = (f32[2048,256]{1,0:T(8,128)}) conditional(s32[]{:T(128)} %bitcast.41, () %tuple.57, (s32[1,1,1,2]{3,2,1,0:T(1,128)S(1)}, bf16[2048,256]{1,0:T(8,128)(2,1)S(1)}, bf16[1,1,1,2,128,128,128]{6,5,4,3,2,1,0:T(8,128)(2,1)}, s32[1,1,1,2]{3,2,1,0:T(1,128)S(1)}, bf16[512,256]{1,0:T(8,128)(2,1)S(1)}, ...), branch_computations={%region_15.18_spmd, %region_16.19_spmd} | conditional | flops 1082130432 | bytes 83099800 | solution.py:139
  499.4 2.5 slice.84
  501.9 3.6 convolution_bitcast_fusion.2
  505.5 6.7 copy.55
  512.4 8.3 multiply_reduce_fusion.2
  523.1 3.7 gather_fusion.3
  526.8 150.8 %all-reduce.5.cloned.1.call-done = f32[256,256]{0,1:T(8,128)} async-done(((f32[256,256]{0,1:T(8,128)}), f32[256,256]{0,1:T(8,128)}) %all-reduce.5.cloned.1.call-update) | async-done | bytes 262160 | tf_op jit(solution)/shard_map/psum | solution.py:115
  678.8 11.7 %cholesky.164 = f32[128,128]{1,0:T(8,128)S(1)} custom-call(f32[128,128]{1,0:T(8,128)S(1)} %cholesky.197), custom_call_target="Cholesky" | custom-call | tf_op jit(solution)/shard_map/jit(cholesky)/cholesky | solution.py:10
  690.6 9.8 %custom-call.17 = f32[1,128,128]{1,2,0:T(8,128)S(1)} custom-call(f32[1,128,128]{2,1,0:T(8,128)S(1)} %get-tuple-element.151), custom_call_target="InvertDiagBlocksLowerTriangular" | custom-call | tf_op jit(solution)/shard_map/jit(cholesky)/cholesky | solution.py:10
  700.9 11.7 %cholesky.181 = f32[128,128]{1,0:T(8,128)S(1)} custom-call(f32[128,128]{1,0:T(8,128)S(1)} %convolution_subtract_fusion), custom_call_target="Cholesky" | custom-call | tf_op jit(solution)/shard_map/jit(cholesky)/cholesky | solution.py:10
  715.2 4.2 while.5
  719.4 19.7 %custom-call.18 = f32[2,128,128]{1,2,0:T(8,128)S(1)} custom-call(f32[2,128,128]{2,1,0:T(8,128)S(1)} %get-tuple-element.125), custom_call_target="InvertDiagBlocksLowerTriangular" | custom-call | tf_op jit(solution)/shard_map/jit(_cho_solve)/triangular_solve | solution.py:11
  742.0 77.3 %psum.39 = f32[256]{0:T(256)S(1)} all-reduce(f32[256]{0:T(256)S(1)} %multiply_reduce_fusion.4), channel_id=1, replica_groups=mesh['ia'=4,'ja'=4,'ka'=16] {'ia','ja','ka'}, use_global_device_ids=true, to_apply=%region_22.25 | all-reduce | flops 256 | bytes 2048 | tf_op jit(solution)/shard_map/psum | solution.py:145
  (109 shorter events, 31.6 us)
Async XLA Ops:
  8.0 85.0 %all-gather.4.cloned.1.call-start = ((), (), s32[]{:S(2)}) async-start(), calls=%async_computation.2 | async-start | bytes 1064960 | tf_op jit(solution)/shard_map/all_gather | solution.py:80
  9.4 262.2 %all-reduce.7.cloned.1.call-start = ((), (), s32[]{:S(2)}) async-start(), calls=%async_computation.7 | async-start | bytes 1048576 | tf_op jit(solution)/shard_map/psum | solution.py:79
  13.5 329.6 %reduce-scatter.3.cloned.1.call-start = ((), (), s32[]{:S(2)}) async-start(), calls=%async_computation.3 | async-start | bytes 2129920 | tf_op jit(solution)/shard_map/reduce_scatter | solution.py:109
  100.7 6.7 copy-start.4
  107.5 8.4 %copy-start.7 = (s32[1,1,1,2]{3,2,1,0:T(1,128)S(1)}, s32[1,1,1,2]{3,2,1,0:T(1,128)}, u32[]{:S(2)}) copy-start(s32[1,1,1,2]{3,2,1,0:T(1,128)} %get-tuple-element.85) | copy-start | bytes 28 | tf_op jit(solution)/shard_map/cond
  121.7 302.8 %copy-start.1 = (s32[64]{0:T(128)S(1)}, s32[64]{0:T(128)}, u32[]{:S(2)}) copy-start(s32[64]{0:T(128)} %param.25) | copy-start | bytes 772
  121.8 375.7 %all-gather.6.cloned.1.call-start = ((), (), s32[]{:S(2)}) async-start(), calls=%async_computation.6 | async-start | bytes 1064960 | tf_op jit(solution)/shard_map/all_gather | solution.py:116
  271.6 227.7 %copy-start.2 = (s32[1,1,1,2]{3,2,1,0:T(1,128)S(1)}, s32[1,1,1,2]{3,2,1,0:T(1,128)}, u32[]{:S(2)}) copy-start(s32[1,1,1,2]{3,2,1,0:T(1,128)} %param.23) | copy-start | bytes 28
  271.6 227.7 %copy-start.3 = (s32[1,1,1,2]{3,2,1,0:T(1,128)S(1)}, s32[1,1,1,2]{3,2,1,0:T(1,128)}, u32[]{:S(2)}) copy-start(s32[1,1,1,2]{3,2,1,0:T(1,128)} %param.22) | copy-start | bytes 28
  271.6 227.7 %copy-start.6 = (s32[1,1,1,2]{3,2,1,0:T(1,128)S(1)}, s32[1,1,1,2]{3,2,1,0:T(1,128)}, u32[]{:S(2)}) copy-start(s32[1,1,1,2]{3,2,1,0:T(1,128)} %param.21) | copy-start | bytes 28
  424.5 253.1 %all-reduce.5.cloned.1.call-start = ((), (), s32[]{:S(2)}) async-start(), calls=%async_computation.4 | async-start | bytes 524288 | tf_op jit(solution)/shard_map/psum | solution.py:115
  425.8 313.4 %reduce-scatter.5.cloned.1.call-start = ((), (), s32[]{:S(2)}) async-start(), calls=%async_computation.5 | async-start | bytes 2129920 | tf_op jit(solution)/shard_map/reduce_scatter | solution.py:143
  523.1 154.5 %copy-start = (f32[256,256]{0,1:T(8,128)S(1)}, f32[256,256]{0,1:T(8,128)}, u32[]{:S(2)}) copy-start(f32[256,256]{0,1:T(8,128)} %get-tuple-element.143) | copy-start | bytes 786436
Sparse Core Ops, SparseCore 0:
  12.2 80.7 all-gather.3
  121.9 159.1 reduce-scatter.2
  424.6 72.8 all-gather.5
  527.0 159.5 reduce-scatter.4
Sparse Core Ops, SparseCore 1:
  15.6 256.0 all-reduce.6
  431.3 246.2 all-reduce.4
where the time goes:
time: 837 us; the launch traced here: 827 us
  waiting for transfers between devices  448 us (54%)
  blocking collectives  155 us (19%)
  other arithmetic  133 us (16%)
  local copies, waits for them, and re-layouts  42.5 us (5%)
  between operations  19.3 us (2%)
  matrix products  17.4 us (2%)
  loops' own time  12.2 us (1%)
    psum x1, waiting for transfers between devices, body(): gram_a = lax.psum(local_a, ('ia', 'ja', 'ka'))  151 us
    psum x1, waiting for transfers between devices, body(): gram_b, gram_c = lax.psum((local_b, local_c), ('ia', 'ja', 'ka'))  150 us
    psum x1, blocking collectives, body(): squares_a = lax.psum(jnp.sum(a_hat * a_hat, axis=0), ('ia', 'ja', 'ka'))  77.9 us
    psum x1, blocking collectives, body(): squares_b = lax.psum(jnp.sum(b_hat * b_hat, axis=0), ('ia', 'ja', 'ka'))  77.3 us
    all_gather x1, waiting for transfers between devices, body(): lax.all_gather(factor_b.astype(jnp.bfloat16), ('ia', 'ka'), axis=1, tiled...  75.5 us
    all_gather x1, waiting for transfers between devices, body(): lax.all_gather(a_own.astype(jnp.bfloat16)[None], ('ja', 'ka'), axis=1, ti...  71.7 us
    another operation x13, other arithmetic, solve_rows(): lower = jnp.linalg.cholesky(gram)  68.6 us
    another operation x5, other arithmetic, solve_rows(): return jax.scipy.linalg.cho_solve((lower, True), rows.T).T  39.4 us
  transfers between devices with their start and end apart: 6, of which 4 were waited for; matrix products, arithmetic and copies ran while one was open for 22% of the time, Pallas kernels for 0%

commit v1 on v0

--- a/solution.py
+++ b/solution.py
@@ -112,7 +112,8 @@
     scale_a = jnp.sqrt(squares_a / total_one + EPS)
     a_own = a_hat / scale_a
     local_a = jnp.dot(a_own.T, a_own, precision=highest, preferred_element_type=jnp.float32)
-    gram_a = lax.psum(local_a, ("ia", "ja", "ka"))
+    pieces = lax.all_gather(local_a, ("ia", "ja", "ka"))
+    gram_a = jnp.sum(pieces, axis=0)
     stored_a = lax.all_gather(a_own.astype(jnp.bfloat16)[None], ("ja", "ka"), axis=1, tiled=True)[0]
     half_a = to_logical(stored_a, owner_one, piece_rows)
 

time: 837 us -> 949 us (1.13)
  waiting for transfers between devices: 448 us -> 537 us
  other arithmetic: 133 us -> 153 us
    all_gather x0 -> x1, waiting for transfers between devices: none -> 185 us  [body(): pieces = lax.all_gather(local_a, ('ia', 'ja', 'ka'))]
    psum x1 -> x0, waiting for transfers between devices: 151 us -> none  [body(): gram_a = lax.psum(local_a, ('ia', 'ja', 'ka'))]
    reduce_scatter x1, waiting for transfers between devices: 0.02 us -> 54.5 us  [body(): lax.psum_scatter(stored_two, ('ia', 'ka'), scatter_dimension=0, tiled=True)]
    reduce_sum x0 -> x1, other arithmetic: none -> 21.3 us  [body(): gram_a = jnp.sum(pieces, axis=0)]
  transfers between devices with their start and end apart: 6 -> 6, of which waited for: 4 -> 5; matrix products, arithmetic and copies ran while one was open for 22% -> 22% of each run, Pallas kernels for 0% -> 0%
where the time goes in v1:
time: 949 us; the launch traced here: 939 us
  waiting for transfers between devices  537 us (57%)
  blocking collectives  157 us (17%)
  other arithmetic  153 us (16%)
  local copies, waits for them, and re-layouts  42.9 us (5%)
  between operations  19.4 us (2%)
  matrix products  17.1 us (2%)
  loops' own time  11.8 us (1%)
    all_gather x1, waiting for transfers between devices, body(): pieces = lax.all_gather(local_a, ('ia', 'ja', 'ka'))  185 us
    psum x1, waiting for transfers between devices, body(): gram_b, gram_c = lax.psum((local_b, local_c), ('ia', 'ja', 'ka'))  150 us
    psum x1, blocking collectives, body(): squares_b = lax.psum(jnp.sum(b_hat * b_hat, axis=0), ('ia', 'ja', 'ka'))  79.8 us
    psum x1, blocking collectives, body(): squares_a = lax.psum(jnp.sum(a_hat * a_hat, axis=0), ('ia', 'ja', 'ka'))  77.6 us
    all_gather x1, waiting for transfers between devices, body(): lax.all_gather(factor_b.astype(jnp.bfloat16), ('ia', 'ka'), axis=1, tiled...  75.5 us
    all_gather x1, waiting for transfers between devices, body(): lax.all_gather(a_own.astype(jnp.bfloat16)[None], ('ja', 'ka'), axis=1, ti...  72 us
    another operation x13, other arithmetic, solve_rows(): lower = jnp.linalg.cholesky(gram)  68.7 us
    reduce_scatter x1, waiting for transfers between devices, body(): lax.psum_scatter(stored_two, ('ia', 'ka'), scatter_dimension=0, tiled=True)  54.5 us
  transfers between devices with their start and end apart: 6, of which 5 were waited for; matrix products, arithmetic and copies ran while one was open for 22% of the time, Pallas kernels for 0%

profile of v1, /device:TPU:1, one launch (start us, length us, event | category | flops | bytes accessed | tf_op | source)
XLA Modules:
  0.0 939.4 jit_solution(7777731737193609385)
XLA Ops:
  9.5 2.0 fusion.34
  11.5 2.0 fusion.36
  17.5 75.5 %all-gather.6.cloned.1.call-done = bf16[1,2048,256]{2,1,0:T(8,128)(2,1)} async-done(((bf16[1,32,256]{2,1,0:T(8,128)(2,1)}), bf16[1,2048,256]{2,1,0:T(8,128)(2,1)}) %all-gather.6.cloned.1.call-update) | async-done | bytes 1048592 | tf_op jit(solution)/shard_map/all_gather | solution.py:80
  94.8 23.3 %conditional.4 = (f32[2048,256]{1,0:T(8,128)}) conditional(s32[]{:T(128)} %bitcast.41, () %tuple.54, (s32[1,1,1,2]{3,2,1,0:T(1,128)}, bf16[512,256]{1,0:T(8,128)(2,1)S(1)}, bf16[1,1,1,2,128,128,128]{6,5,4,3,2,1,0:T(8,128)(2,1)}, s32[1,1,1,2]{3,2,1,0:T(1,128)}, bf16[2048,256]{1,0:T(8,128)(2,1)S(1)}, /*index=5*/s32[1,1,1,2]{3,2,1,0:T(1,128)}) %tuple.134), branch_computations={%region_6.0_spmd, %region_7.0_spmd} | conditional | flops 1082130432 | bytes 83099928 | solution.py:104
  95.5 2.8 slice.76
  98.3 2.4 convolution_bitcast_fusion
  100.7 6.7 copy.55
  107.6 8.2 multiply_reduce_fusion
  118.1 3.6 gather_fusion.1
  122.1 149.5 %all-reduce.4.cloned.1.call-done = (f32[256,256]{0,1:T(8,128)}, f32[256,256]{0,1:T(8,128)}) async-done(((f32[256,256]{0,1:T(8,128)}, f32[256,256]{0,1:T(8,128)}), (f32[256,256]{0,1:T(8,128)}, f32[256,256]{0,1:T(8,128)})) %all-reduce.4.cloned.1.call-update) | async-done | bytes 524304 | tf_op jit(solution)/shard_map/psum | solution.py:79
  272.9 11.7 %cholesky.130 = f32[128,128]{1,0:T(8,128)S(1)} custom-call(f32[128,128]{1,0:T(8,128)S(1)} %cholesky.194), custom_call_target="Cholesky" | custom-call | tf_op jit(solution)/shard_map/jit(cholesky)/cholesky | solution.py:10
  284.6 9.8 %custom-call.15 = f32[1,128,128]{1,2,0:T(8,128)S(1)} custom-call(f32[1,128,128]{2,1,0:T(8,128)S(1)} %get-tuple-element.155), custom_call_target="InvertDiagBlocksLowerTriangular" | custom-call | tf_op jit(solution)/shard_map/jit(cholesky)/cholesky | solution.py:10
  295.0 11.7 %cholesky.147 = f32[128,128]{1,0:T(8,128)S(1)} custom-call(f32[128,128]{1,0:T(8,128)S(1)} %convolution_subtract_fusion.1), custom_call_target="Cholesky" | custom-call | tf_op jit(solution)/shard_map/jit(cholesky)/cholesky | solution.py:10
  308.9 14.6 %while.4 = (s32[]{:T(128)}, f32[256,256]{1,0:T(8,128)S(1)}, s32[2,2]{1,0:T(2,128)S(1)}, f32[2,128,128]{2,1,0:T(8,128)S(1)}, s32[]{:T(128)}) while((s32[]{:T(128)}, f32[256,256]{1,0:T(8,128)S(1)}, s32[2,2]{1,0:T(2,128)S(1)}, f32[2,128,128]{2,1,0:T(8,128)S(1)}, s32[]{:T(128)}) %tuple.103), condition=%wide.while_cond, body=%wide.while_body.sunk | while | flops 2 | bytes 131181 | solution.py:11
  323.5 19.7 %custom-call.16 = f32[2,128,128]{1,2,0:T(8,128)S(1)} custom-call(f32[2,128,128]{2,1,0:T(8,128)S(1)} %get-tuple-element.124), custom_call_target="InvertDiagBlocksLowerTriangular" | custom-call | tf_op jit(solution)/shard_map/jit(_cho_solve)/triangular_solve | solution.py:11
  345.8 77.6 %psum.30 = f32[256]{0:T(256)S(1)} all-reduce(f32[256]{0:T(256)S(1)} %multiply_reduce_fusion.5), channel_id=1, replica_groups=mesh['ia'=4,'ja'=4,'ka'=16] {'ia','ja','ka'}, use_global_device_ids=true, to_apply=%region_13.16 | all-reduce | flops 256 | bytes 2048 | tf_op jit(solution)/shard_map/psum | solution.py:111
  425.4 72.0 %all-gather.10.cloned.1.call-done = bf16[2048,256]{1,0:T(8,128)(2,1)} async-done(((bf16[32,256]{1,0:T(8,128)(2,1)}), bf16[2048,256]{1,0:T(8,128)(2,1)}) %all-gather.10.cloned.1.call-update) | async-done | bytes 1048592 | tf_op jit(solution)/shard_map/all_gather | solution.py:117
  499.2 23.7 %conditional.6 = (f32[2048,256]{1,0:T(8,128)}) conditional(s32[]{:T(128)} %bitcast.41, () %tuple.57, (s32[1,1,1,2]{3,2,1,0:T(1,128)S(1)}, bf16[2048,256]{1,0:T(8,128)(2,1)S(1)}, bf16[1,1,1,2,128,128,128]{6,5,4,3,2,1,0:T(8,128)(2,1)}, s32[1,1,1,2]{3,2,1,0:T(1,128)S(1)}, bf16[512,256]{1,0:T(8,128)(2,1)S(1)}, ...), branch_computations={%region_15.18_spmd, %region_16.19_spmd} | conditional | flops 1082130432 | bytes 83099800 | solution.py:140
  499.3 2.5 slice.84
  501.8 3.6 convolution_bitcast_fusion.2
  505.4 6.8 copy.58
  512.3 8.4 multiply_reduce_fusion.2
  523.2 3.6 gather_fusion.3
  526.8 185.1 %all-gather.8.cloned.1.call-done = f32[65536,256]{1,0:T(8,128)} async-done(((f32[256,256]{1,0:T(8,128)}), f32[65536,256]{1,0:T(8,128)}) %all-gather.8.cloned.1.call-update) | async-done | bytes 67108880 | tf_op jit(solution)/shard_map/all_gather | solution.py:115
  711.9 21.3 %reduce_sum.52 = f32[256,256]{1,0:T(8,128)S(1)} reduce(f32[256,256,256]{2,1,0:T(8,128)} %bitcast.52, f32[]{:T(128)} %constant.148.clone.1), dimensions={0}, to_apply=%region_14.17 | reduce | flops 16711680 | bytes 67371008 | tf_op jit(solution)/shard_map/reduce_sum | solution.py:116
  733.6 11.7 %cholesky.164 = f32[128,128]{1,0:T(8,128)S(1)} custom-call(f32[128,128]{1,0:T(8,128)S(1)} %cholesky.197), custom_call_target="Cholesky" | custom-call | tf_op jit(solution)/shard_map/jit(cholesky)/cholesky | solution.py:10
  745.4 9.8 %custom-call.17 = f32[1,128,128]{1,2,0:T(8,128)S(1)} custom-call(f32[1,128,128]{2,1,0:T(8,128)S(1)} %get-tuple-element.151), custom_call_target="InvertDiagBlocksLowerTriangular" | custom-call | tf_op jit(solution)/shard_map/jit(cholesky)/cholesky | solution.py:10
  755.7 11.7 %cholesky.181 = f32[128,128]{1,0:T(8,128)S(1)} custom-call(f32[128,128]{1,0:T(8,128)S(1)} %convolution_subtract_fusion), custom_call_target="Cholesky" | custom-call | tf_op jit(solution)/shard_map/jit(cholesky)/cholesky | solution.py:10
  770.1 4.1 while.5
  774.3 19.9 %custom-call.18 = f32[2,128,128]{1,2,0:T(8,128)S(1)} custom-call(f32[2,128,128]{2,1,0:T(8,128)S(1)} %get-tuple-element.125), custom_call_target="InvertDiagBlocksLowerTriangular" | custom-call | tf_op jit(solution)/shard_map/jit(_cho_solve)/triangular_solve | solution.py:11
  794.2 54.5 %reduce-scatter.5.cloned.1.call-done = f32[32,256]{1,0:T(8,128)} async-done(((f32[2048,256]{1,0:T(8,128)}), f32[32,256]{1,0:T(8,128)}) %reduce-scatter.5.cloned.1.call-update) | async-done | bytes 32784 | tf_op jit(solution)/shard_map/reduce_scatter | solution.py:144
  851.4 79.8 %psum.31 = f32[256]{0:T(256)S(1)} all-reduce(f32[256]{0:T(256)S(1)} %multiply_reduce_fusion.4), channel_id=1, replica_groups=mesh['ia'=4,'ja'=4,'ka'=16] {'ia','ja','ka'}, use_global_device_ids=true, to_apply=%region_22.25 | all-reduce | flops 256 | bytes 2048 | tf_op jit(solution)/shard_map/psum | solution.py:146
  (111 shorter events, 34.4 us)
Async XLA Ops:
  8.0 85.0 %all-gather.6.cloned.1.call-start = ((), (), s32[]{:S(2)}) async-start(), calls=%async_computation.2 | async-start | bytes 1064960 | tf_op jit(solution)/shard_map/all_gather | solution.py:80
  9.4 262.2 %all-reduce.4.cloned.1.call-start = ((), (), s32[]{:S(2)}) async-start(), calls=%async_computation.7 | async-start | bytes 1048576 | tf_op jit(solution)/shard_map/psum | solution.py:79
  13.4 329.7 %reduce-scatter.3.cloned.1.call-start = ((), (), s32[]{:S(2)}) async-start(), calls=%async_computation.3 | async-start | bytes 2129920 | tf_op jit(solution)/shard_map/reduce_scatter | solution.py:109
  100.7 6.7 copy-start.4
  107.5 8.4 copy-start.7
  121.7 303.6 %copy-start.1 = (s32[64]{0:T(128)S(1)}, s32[64]{0:T(128)}, u32[]{:S(2)}) copy-start(s32[64]{0:T(128)} %param.25) | copy-start | bytes 772
  121.8 377.5 %copy-start.2 = (s32[1,1,1,2]{3,2,1,0:T(1,128)S(1)}, s32[1,1,1,2]{3,2,1,0:T(1,128)}, u32[]{:S(2)}) copy-start(s32[1,1,1,2]{3,2,1,0:T(1,128)} %param.23) | copy-start | bytes 28
  121.8 377.4 %copy-start.3 = (s32[1,1,1,2]{3,2,1,0:T(1,128)S(1)}, s32[1,1,1,2]{3,2,1,0:T(1,128)}, u32[]{:S(2)}) copy-start(s32[1,1,1,2]{3,2,1,0:T(1,128)} %param.22) | copy-start | bytes 28
  121.8 377.4 %copy-start.6 = (s32[1,1,1,2]{3,2,1,0:T(1,128)S(1)}, s32[1,1,1,2]{3,2,1,0:T(1,128)}, u32[]{:S(2)}) copy-start(s32[1,1,1,2]{3,2,1,0:T(1,128)} %param.21) | copy-start | bytes 28
  121.8 375.6 %all-gather.10.cloned.1.call-start = ((), (), s32[]{:S(2)}) async-start(), calls=%async_computation.6 | async-start | bytes 1064960 | tf_op jit(solution)/shard_map/all_gather | solution.py:117
  424.1 287.8 %all-gather.8.cloned.1.call-start = ((), (), s32[]{:S(2)}) async-start(), calls=%async_computation.5 | async-start | bytes 67371008 | tf_op jit(solution)/shard_map/all_gather | solution.py:115
  425.3 423.4 %reduce-scatter.5.cloned.1.call-start = ((), (), s32[]{:S(2)}) async-start(), calls=%async_computation.4 | async-start | bytes 2129920 | tf_op jit(solution)/shard_map/reduce_scatter | solution.py:144
  711.9 21.4 %copy-start = (f32[256,256]{0,1:T(8,128)S(1)}, f32[256,256]{0,1:T(8,128)}, u32[]{:S(2)}) copy-start(f32[256,256]{0,1:T(8,128)} %get-tuple-element.143) | copy-start | bytes 786436
Sparse Core Ops, SparseCore 0:
  12.2 80.7 all-gather.5
  121.9 159.1 reduce-scatter.2
  424.2 73.0 all-gather.9
  501.6 210.3 all-gather.7
  716.4 132.3 reduce-scatter.4
Sparse Core Ops, SparseCore 1:
  15.6 256.0 all-reduce.3
